TPU v7x, 32 devices: a whole 2x2x4 slice. The times are simulated.
32 devices in a mesh: scan: 8 (over z, x), bin: 4 (over y, core).
Axes of the slice: x: 2, y: 2, z: 4, core: 2. Of those that a mesh axis runs over, the one named last changes fastest.
Arguments:
- tile_blocks: bfloat16 [64, 16, 256, 256], P('scan', 'bin'), may hold values from -0.25 to 0.25
- tile_pattern: int32 [2, 64], P(None, 'scan'), may hold values from 0 to 63, as said below
- tile_count: int32 [8], P('scan'), may hold values from 1 to 8, as said below
- initial_map: float32 [16, 4, 4096], P('bin', None, 'scan')
- measured: float32 [16, 4, 16384], P('bin', None, 'scan')
- step_size: float32 [1], replicated, may hold values from 0.06 to 0.1
- penalty: float32 [4096], P('scan'), may hold values from 40 to 200
Outputs:
- source_map: float32 [16, 4, 4096], P('bin', None, 'scan')
Inputs may be any that keep to these rules, and one draw needn't show every extreme that they name: `tile_pattern`: row 0 names a sensor block of 64; row 1 of slot s names one of the 2 scan tiles (s // 8) * 2 to (s // 8) * 2 + 1. Only the first tile_count[d] slots of index d of scan are live; in every draw some indices have all 8 slots live.
All inputs are finite; a program needn't handle non-finite values.
Results may differ from a plain program's by a relative error of at most 0.00074.
Values may be sent and summed in bfloat16 or wider, within the bound.
No kernel may reach another device: no remote copies, remote signals or barrier semaphores. Data moves between devices by JAX's collectives and lax.ppermute only.
A program may use at most 64 MiB of HBM per device.

v0:
```python
import jax
import jax.numpy as jnp
from jax import lax
from jax.sharding import PartitionSpec as P

ITERS = 2


def add_forward(partial_value, tile_set, block_rows, block_cols, points, first_slot, end_slot):
    tile_width = tile_set.shape[-1]

    def advance(slot_id, running):
        matrix = lax.dynamic_index_in_dim(tile_set, slot_id, 0, keepdims=False)
        source = lax.dynamic_slice_in_dim(points, block_cols[slot_id] * tile_width, tile_width, 2)
        contrib = jnp.einsum("fij,fsj->fsi", matrix, source, preferred_element_type=jnp.float32)
        start = block_rows[slot_id] * tile_width
        present = lax.dynamic_slice_in_dim(running, start, tile_width, 2)
        return lax.dynamic_update_slice_in_dim(running, present + contrib, start, 2)

    return lax.fori_loop(first_slot, end_slot, advance, partial_value)


def add_backward(gradient, tile_set, block_rows, block_cols, residual, first_slot, end_slot):
    tile_width = tile_set.shape[-1]

    def advance(slot_id, running):
        matrix = lax.dynamic_index_in_dim(tile_set, slot_id, 0, keepdims=False)
        source = lax.dynamic_slice_in_dim(residual, block_rows[slot_id] * tile_width, tile_width, 2)
        contrib = jnp.einsum("fij,fsi->fsj", matrix, source, preferred_element_type=jnp.float32)
        start = block_cols[slot_id] * tile_width
        present = lax.dynamic_slice_in_dim(running, start, tile_width, 2)
        return lax.dynamic_update_slice_in_dim(running, present + contrib, start, 2)

    return lax.fori_loop(first_slot, end_slot, advance, gradient)


def home_slots(rows, tile_width, sensors_dev, homed):
    return rows * tile_width // sensors_dev * homed + rows % homed


def body(tile_blocks, tile_pattern, tile_count, initial_map, measured, step_size, penalty):
    tile_width = tile_blocks.shape[-1]
    per_device = initial_map.shape[2] // tile_width
    block_rows = tile_pattern[0]
    block_cols = tile_pattern[1] - lax.axis_index("scan") * per_device
    live_count = tile_count[0]
    bins_dev, snapshots, sensors_dev = measured.shape
    scan_count = lax.axis_size("scan")
    sensors = sensors_dev * scan_count
    homed = max(1, sensors_dev // tile_width)
    measured_all = lax.all_gather(measured, "scan", axis=2, tiled=True)
    block_rows = home_slots(block_rows, tile_width, sensors_dev, homed)
    own_measured = lax.dynamic_slice_in_dim(
        measured_all, lax.axis_index("scan") * sensors_dev, homed * tile_width, 2
    )
    sensors = scan_count * homed * tile_width
    current = initial_map
    for iteration in range(ITERS):
        rounded_map = current.astype(jnp.bfloat16)
        partial_value = jnp.zeros((bins_dev, snapshots, sensors), jnp.float32)
        partial_value = add_forward(
            partial_value, tile_blocks, block_rows, block_cols, rounded_map, 0, live_count
        )
        outgoing = partial_value.reshape(bins_dev, snapshots, scan_count, homed * tile_width)
        arrived = lax.all_to_all(outgoing, "scan", split_axis=2, concat_axis=2, tiled=True)
        totals = jnp.sum(arrived, axis=2)
        rounded = (totals - own_measured).astype(jnp.bfloat16)
        residual = lax.all_gather(rounded, "scan", axis=2, tiled=True)
        gradient = jnp.zeros_like(current)
        gradient = add_backward(
            gradient, tile_blocks, block_rows, block_cols, residual, 0, live_count
        )
        moved = current - step_size[0] * gradient
        energy = lax.psum(jnp.sum(moved * moved, axis=(0, 1)), "bin")
        current = moved * jnp.maximum(0.0, 1.0 - step_size[0] * penalty / jnp.sqrt(energy + 1e-06))
    return current


def solution(mesh):
    in_specs = (
        P("scan", "bin", None, None),
        P(None, "scan"),
        P("scan"),
        P("bin", None, "scan"),
        P("bin", None, "scan"),
        P(),
        P("scan"),
    )
    out_specs = P("bin", None, "scan")
    return jax.shard_map(body, mesh=mesh, in_specs=in_specs, out_specs=out_specs, check_vma=False)
```

profile of v0, /device:TPU:12, one launch (start us, length us, event | category | flops | bytes accessed | tf_op | source)
XLA Modules:
  0.0 327.0 jit_solution(14422891736312756115)
XLA Ops:
  6.5 0.7 fusion.20
  7.2 0.7 subtract_bitcast_fusion
  7.9 0.8 convert_element_type.12
  8.8 38.3 %while.40 = (s32[]{:T(128)}, f32[4,4,16384]{2,1,0:T(4,128)S(1)}, s32[]{:T(128)}, s32[8]{0:T(128)S(1)}, s32[8]{0:T(128)S(1)}, /*index=5*/bf16[4,4,512]{2,1,0:T(4,...) while((s32[]{:T(128)}, f32[4,4,16384]{2,1,0:T(4,128)S(1)}, ...), condition=%wide.region_1.2_spmd, body=%wide.region_0.1_spmd.sunk | while | flops 2101261 | bytes 565535 | solution.py:20
  10.9 0.7 dynamic_slice.118
  12.2 1.3 fusion.36
  15.6 0.7 dynamic_slice.118
  16.9 1.3 fusion.36
  20.3 0.7 dynamic_slice.118
  21.6 1.3 fusion.36
  25.0 0.7 dynamic_slice.118
  26.4 1.3 fusion.36
  29.7 0.7 dynamic_slice.118
  31.1 1.3 fusion.36
  34.4 0.7 dynamic_slice.118
  35.8 1.3 fusion.36
  39.1 0.7 dynamic_slice.118
  40.5 1.3 fusion.36
  43.8 0.7 dynamic_slice.118
  45.2 1.3 fusion.36
  47.2 1.1 copy.15
  48.3 5.5 %all-to-all-start = ((f32[4,4,8,2048]{3,1,0,2:T(4,128)}), f32[4,4,8,2048]{3,1,0,2:T(4,128)S(1)}, u32[]{:S(2)}, u32[]{:S(2)}) async-start(f32[4,4,8,2048]{3,1,0,2:T(4,128)} %bitcast.36), calls=%async_computation | async-start | bytes 2097152 | tf_op jit(solution)/shard_map/all_to_all | solution.py:65
  53.7 0.7 all-gather.2.cloned.1.call-update
  55.1 26.2 %all-to-all-done = f32[4,4,8,2048]{3,1,0,2:T(4,128)S(1)} async-done(((f32[4,4,8,2048]{3,1,0,2:T(4,128)}), f32[4,4,8,2048]{3,1,0,2:T(4,128)S(1)}, u32[]{:S(2)}, u32[]{:S(2)}) %all-to-all-start) | async-done | bytes 1048608 | tf_op jit(solution)/shard_map/all_to_all | solution.py:65
  81.5 20.1 %all-gather.2.cloned.1.call-done = f32[4,4,16384]{2,1,0:T(4,128)} async-done(((f32[4,4,2048]{2,1,0:T(4,128)}), f32[4,4,16384]{2,1,0:T(4,128)}) %all-gather.2.cloned.1.call-update) | async-done | bytes 1048592 | tf_op jit(solution)/shard_map/all_gather | solution.py:51
  101.6 0.9 subtract_convert_fusion.1
  102.6 29.9 %all_gather.10 = bf16[4,4,16384]{2,1,0:T(4,128)(2,1)S(1)} all-gather(bf16[4,4,2048]{2,1,0:T(4,128)(2,1)S(1)} %subtract_convert_fusion.1), channel_id=1, replica_groups=mesh['scan'=8,'bin'=4] {'scan'}, dimensions={2}, use_global_device_ids=true | all-gather | bytes 589824 | tf_op jit(solution)/shard_map/all_gather | solution.py:68
  132.5 37.8 %while.41 = (s32[]{:T(128)}, f32[4,4,512]{2,1,0:T(4,128)S(1)}, s32[]{:T(128)}, s32[8]{0:T(128)S(1)}, s32[8]{0:T(128)S(1)}, /*index=5*/bf16[4,4,16384]{2,1,0:T(4,...) while((s32[]{:T(128)}, f32[4,4,512]{2,1,0:T(4,128)S(1)}, ...), condition=%wide.region_4.5_spmd, body=%wide.region_3.4_spmd.sunk | while | flops 2101261 | bytes 565535 | solution.py:34
  135.9 1.2 fusion.39
  140.5 1.2 fusion.39
  145.2 1.2 fusion.39
  149.8 1.2 fusion.39
  154.5 1.2 fusion.39
  159.1 1.2 fusion.39
  163.7 1.2 fusion.39
  168.4 1.2 fusion.39
  170.3 5.9 %psum.14 = f32[512]{0:T(512)S(1)} all-reduce(f32[512]{0:T(512)S(1)} %get-tuple-element.217), channel_id=1, replica_groups=mesh['scan'=8,'bin'=4] {'bin'}, use_global_device_ids=true, to_apply=%region_6.7 | all-reduce | flops 512 | bytes 4096 | tf_op jit(solution)/shard_map/psum | solution.py:74
  176.4 38.3 %while.42 = (s32[]{:T(128)}, f32[4,4,16384]{2,1,0:T(4,128)S(1)}, s32[]{:T(128)}, s32[8]{0:T(128)S(1)}, s32[8]{0:T(128)S(1)}, /*index=5*/bf16[4,4,512]{2,1,0:T(4,...) while((s32[]{:T(128)}, f32[4,4,16384]{2,1,0:T(4,128)S(1)}, ...), condition=%wide.region_8.9_spmd, body=%wide.region_7.8_spmd.sunk | while | flops 2101261 | bytes 565535 | solution.py:20
  179.8 1.3 fusion.42
  184.5 1.3 fusion.42
  189.2 1.3 fusion.42
  193.9 1.3 fusion.42
  198.6 1.3 fusion.42
  203.3 1.3 fusion.42
  208.0 1.3 fusion.42
  212.7 1.3 fusion.42
  214.7 1.1 copy.14
  215.8 5.1 %all-to-all-start.1 = ((f32[4,4,8,2048]{3,1,0,2:T(4,128)}), f32[4,4,8,2048]{3,1,0,2:T(4,128)S(1)}, u32[]{:S(2)}, u32[]{:S(2)}) async-start(f32[4,4,8,2048]{3,1,0,2:T(4,128)} %bitcast.35), calls=%async_computation.1 | async-start | bytes 2097152 | tf_op jit(solution)/shard_map/all_to_all | solution.py:65
  220.9 23.2 %all-to-all-done.1 = f32[4,4,8,2048]{3,1,0,2:T(4,128)S(1)} async-done(((f32[4,4,8,2048]{3,1,0,2:T(4,128)}), f32[4,4,8,2048]{3,1,0,2:T(4,128)S(1)}, u32[]{:S(2)}, u32[]{:S(2)}) %all-to-all-start.1) | async-done | bytes 1048608 | tf_op jit(solution)/shard_map/all_to_all | solution.py:65
  244.3 0.9 subtract_convert_fusion
  245.2 30.7 %all_gather.11 = bf16[4,4,16384]{2,1,0:T(4,128)(2,1)S(1)} all-gather(bf16[4,4,2048]{2,1,0:T(4,128)(2,1)S(1)} %subtract_convert_fusion), channel_id=1, replica_groups=mesh['scan'=8,'bin'=4] {'scan'}, dimensions={2}, use_global_device_ids=true | all-gather | bytes 589824 | tf_op jit(solution)/shard_map/all_gather | solution.py:68
  275.9 37.8 %while.43 = (s32[]{:T(128)}, f32[4,4,512]{2,1,0:T(4,128)S(1)}, s32[]{:T(128)}, s32[8]{0:T(128)S(1)}, s32[8]{0:T(128)S(1)}, /*index=5*/bf16[4,4,16384]{2,1,0:T(4,...) while((s32[]{:T(128)}, f32[4,4,512]{2,1,0:T(4,128)S(1)}, ...), condition=%wide.region_11.12_spmd, body=%wide.region_10.11_spmd.sunk | while | flops 2101261 | bytes 565535 | solution.py:34
  278.0 0.7 dynamic_slice.133
  279.4 1.2 fusion.45
  282.6 0.7 dynamic_slice.133
  284.0 1.2 fusion.45
  287.3 0.7 dynamic_slice.133
  288.6 1.2 fusion.45
  293.3 1.2 fusion.45
  297.9 1.2 fusion.45
  302.6 1.2 fusion.45
  307.2 1.2 fusion.45
  311.9 1.2 fusion.45
  313.8 5.8 %psum.15 = f32[512]{0:T(512)S(1)} all-reduce(f32[512]{0:T(512)S(1)} %multiply_reduce_fusion), channel_id=1, replica_groups=mesh['scan'=8,'bin'=4] {'bin'}, use_global_device_ids=true, to_apply=%region_13.14 | all-reduce | flops 512 | bytes 4096 | tf_op jit(solution)/shard_map/psum | solution.py:74
  (70 shorter events, 36.7 us)
Async XLA Ops:
  48.3 122.0 %copy-start = (f32[4,4,512]{2,1,0:T(4,128)S(1)}, f32[4,4,512]{2,1,0:T(4,128)}, u32[]{:S(2)}) copy-start(f32[4,4,512]{2,1,0:T(4,128)} %param.18) | copy-start | bytes 98308
  48.3 127.9 %copy-start.1 = (f32[512]{0:T(512)S(1)}, f32[512]{0:T(512)}, u32[]{:S(2)}) copy-start(f32[512]{0:T(512)} %param.21) | copy-start | bytes 6148
  48.3 33.0 %all-to-all-start = ((f32[4,4,8,2048]{3,1,0,2:T(4,128)}), f32[4,4,8,2048]{3,1,0,2:T(4,128)S(1)}, u32[]{:S(2)}, u32[]{:S(2)}) async-start(f32[4,4,8,2048]{3,1,0,2:T(4,128)} %bitcast.36), calls=%async_computation | async-start | bytes 2097152 | tf_op jit(solution)/shard_map/all_to_all | solution.py:65
  53.7 47.9 %all-gather.2.cloned.1.call-start = ((), (), s32[]{:S(2)}) async-start(), calls=%async_computation.2 | async-start | bytes 1179648 | tf_op jit(solution)/shard_map/all_gather | solution.py:51
  215.8 28.3 %all-to-all-start.1 = ((f32[4,4,8,2048]{3,1,0,2:T(4,128)}), f32[4,4,8,2048]{3,1,0,2:T(4,128)S(1)}, u32[]{:S(2)}, u32[]{:S(2)}) async-start(f32[4,4,8,2048]{3,1,0,2:T(4,128)} %bitcast.35), calls=%async_computation.1 | async-start | bytes 2097152 | tf_op jit(solution)/shard_map/all_to_all | solution.py:65
Sparse Core Ops, SparseCore 0:
  56.7 44.8 all-gather.1
where the time goes:
time: 330 us; the launch traced here: 327 us
  blocking collectives  72.3 us (22%)
  waiting for transfers between devices  70.2 us (21%)
  loops' own time  69.3 us (21%)
  local copies, waits for them, and re-layouts  45.2 us (14%)
  matrix products  40.3 us (12%)
  between operations  14.1 us (4%)
  starting transfers between devices  10.5 us (3%)
  other arithmetic  5.18 us (2%)
    all_gather x2, blocking collectives, body(): residual = lax.all_gather(rounded, 'scan', axis=2, tiled=True)  60.6 us
    all_to_all x2, waiting for transfers between devices, body(): lax.all_to_all(outgoing, 'scan', split_axis=2, concat_axis=2, tiled=True)  49.4 us
    another operation x2, loops' own time, add_forward(): return lax.fori_loop(first_slot, end_slot, advance, partial_value)  34.7 us
    another operation x2, loops' own time, add_backward(): return lax.fori_loop(first_slot, end_slot, advance, gradient)  34.5 us
    dot_general x16, matrix products, advance(): jnp.einsum('fij,fsj->fsi', matrix, source, preferred_element_type=jnp.flo...  20.6 us
    all_gather x1, waiting for transfers between devices, body(): measured_all = lax.all_gather(measured, 'scan', axis=2, tiled=True)  20.1 us
    dot_general x16, matrix products, advance(): jnp.einsum('fij,fsi->fsj', matrix, source, preferred_element_type=jnp.flo...  19.7 us
    psum x2, blocking collectives, body(): energy = lax.psum(jnp.sum(moved * moved, axis=(0, 1)), 'bin')  11.7 us
  transfers between devices with their start and end apart: 3, of which 3 were waited for; matrix products, arithmetic and copies ran while one was open for 0% of the time, Pallas kernels for 0%

commit v1 on v0

--- a/solution.py
+++ b/solution.py
@@ -4,6 +4,12 @@
 from jax.sharding import PartitionSpec as P
 
 ITERS = 2
+
+
+def in_order(parts, dim):
+    shape = list(parts.shape[1:])
+    shape[dim] *= parts.shape[0]
+    return jnp.moveaxis(parts, 0, dim).reshape(shape)
 
 
 def add_forward(partial_value, tile_set, block_rows, block_cols, points, first_slot, end_slot):
@@ -48,7 +54,14 @@
     scan_count = lax.axis_size("scan")
     sensors = sensors_dev * scan_count
     homed = max(1, sensors_dev // tile_width)
-    measured_all = lax.all_gather(measured, "scan", axis=2, tiled=True)
+    devices = lax.axis_size("scan")
+    right = [(i, (i + 1) % devices) for i in range(devices)]
+    parts = [measured]
+    while len(parts) < devices:
+        parts.append(lax.ppermute(parts[-1], "scan", right))
+    index = lax.axis_index("scan")
+    parts = jnp.stack(parts)[(index - jnp.arange(devices)) % devices]
+    measured_all = in_order(parts, 2)
     block_rows = home_slots(block_rows, tile_width, sensors_dev, homed)
     own_measured = lax.dynamic_slice_in_dim(
         measured_all, lax.axis_index("scan") * sensors_dev, homed * tile_width, 2

time: 330 us -> 325 us (0.985)
  starting transfers between devices: 10.5 us -> 32 us
  between operations: 14.1 us -> 0.84 us
  waiting for transfers between devices: 70.2 us -> 57.6 us
  blocking collectives: 72.3 us -> 79 us
  loops' own time: 69.3 us -> 65.7 us
    ppermute x0 -> x7, waiting for transfers between devices: none -> 34.4 us  [body(): parts.append(lax.ppermute(parts[-1], 'scan', right))]
    all_to_all x2, waiting for transfers between devices: 49.4 us -> 23.2 us  [body(): lax.all_to_all(outgoing, 'scan', split_axis=2, concat_axis=2, tiled=True)]
    ppermute x0 -> x7, starting transfers between devices: none -> 21.8 us  [body(): parts.append(lax.ppermute(parts[-1], 'scan', right))]
    all_gather x1 -> x0, waiting for transfers between devices: 20.1 us -> none  [body(): measured_all = lax.all_gather(measured, 'scan', axis=2, tiled=True)]
    all_gather x2, blocking collectives: 60.6 us -> 67.3 us  [body(): residual = lax.all_gather(rounded, 'scan', axis=2, tiled=True)]
  transfers between devices with their start and end apart: 3 -> 9, of which waited for: 3 -> 7; matrix products, arithmetic and copies ran while one was open for 0% -> 8% of each run, Pallas kernels for 0% -> 0%
where the time goes in v1:
time: 325 us; the launch traced here: 322 us
  blocking collectives  79 us (24%)
  loops' own time  65.7 us (20%)
  waiting for transfers between devices  57.6 us (18%)
  local copies, waits for them, and re-layouts  43.1 us (13%)
  matrix products  40.3 us (12%)
  starting transfers between devices  32 us (10%)
  other arithmetic  3.4 us (1%)
    all_gather x2, blocking collectives, body(): residual = lax.all_gather(rounded, 'scan', axis=2, tiled=True)  67.3 us
    ppermute x7, waiting for transfers between devices, body(): parts.append(lax.ppermute(parts[-1], 'scan', right))  34.4 us
    another operation x2, loops' own time, add_forward(): return lax.fori_loop(first_slot, end_slot, advance, partial_value)  32.9 us
    another operation x2, loops' own time, add_backward(): return lax.fori_loop(first_slot, end_slot, advance, gradient)  32.7 us
    all_to_all x2, waiting for transfers between devices, body(): lax.all_to_all(outgoing, 'scan', split_axis=2, concat_axis=2, tiled=True)  23.2 us
    ppermute x7, starting transfers between devices, body(): parts.append(lax.ppermute(parts[-1], 'scan', right))  21.8 us
    dot_general x16, matrix products, advance(): jnp.einsum('fij,fsj->fsi', matrix, source, preferred_element_type=jnp.flo...  20.6 us
    dot_general x16, matrix products, advance(): jnp.einsum('fij,fsi->fsj', matrix, source, preferred_element_type=jnp.flo...  19.7 us
  transfers between devices with their start and end apart: 9, of which 7 were waited for; matrix products, arithmetic and copies ran while one was open for 8% of the time, Pallas kernels for 0%

profile of v1, /device:TPU:12, one launch (start us, length us, event | category | flops | bytes accessed | tf_op | source)
XLA Modules:
  0.0 321.8 jit_solution(9401226454658368087)
XLA Ops:
  0.0 1.5 collective-permute-start
  1.5 0.7 fusion.20
  2.2 0.7 subtract_bitcast_fusion
  2.9 0.8 convert_element_type.12
  3.8 36.6 %while.40 = (s32[]{:T(128)}, f32[4,4,16384]{2,1,0:T(4,128)S(1)}, s32[]{:T(128)}, s32[8]{0:T(128)S(1)}, s32[8]{0:T(128)S(1)}, /*index=5*/bf16[4,4,512]{2,1,0:T(4,...) while((s32[]{:T(128)}, f32[4,4,16384]{2,1,0:T(4,128)S(1)}, ...), condition=%wide.region_1.2_spmd, body=%wide.region_0.1_spmd.sunk | while | flops 2101261 | bytes 565535 | solution.py:26
  7.0 1.3 fusion.38
  11.5 1.3 fusion.38
  16.0 1.3 fusion.38
  20.4 1.3 fusion.38
  24.9 1.3 fusion.38
  29.4 1.3 fusion.38
  33.9 1.3 fusion.38
  38.4 1.3 fusion.38
  40.4 1.0 copy.19
  41.4 5.3 %all-to-all-start = ((f32[4,4,8,2048]{3,1,0,2:T(4,128)}), f32[4,4,8,2048]{3,1,0,2:T(4,128)S(1)}, u32[]{:S(2)}, u32[]{:S(2)}) async-start(f32[4,4,8,2048]{3,1,0,2:T(4,128)} %bitcast.57), calls=%async_computation | async-start | bytes 2097152 | tf_op jit(solution)/shard_map/all_to_all | solution.py:78
  47.5 1.5 collective-permute-start.1
  49.0 19.0 %collective-permute-done.1 = f32[4,4,2048]{2,1,0:T(4,128)S(1)} collective-permute-done((f32[4,4,2048]{2,1,0:T(4,128)S(1)}, f32[4,4,2048]{2,1,0:T(4,128)S(1)}, u32[]{:S(2)}, u32[]{:S(2)}) %collective-permute-start.1) | collective-permute-done | bytes 131104 | tf_op jit(solution)/shard_map/ppermute | solution.py:61
  68.0 5.2 %collective-permute-start.2 = (f32[4,4,2048]{2,1,0:T(4,128)S(1)}, f32[4,4,2048]{2,1,0:T(4,128)S(1)}, u32[]{:S(2)}, u32[]{:S(2)}) collective-permute-start(f32[4,4,2048]{2,1,0:T(4,128)S(1)} %collective-permute-done.1), channel_id=1, source_target_pairs={{0,4},{4,8},{8,12},{12,16},{16,20},{20,24},{24,28},{28,0},{1,5},{5... | collective-permute-start | bytes 393224 | tf_op jit(solution)/shard_map/ppermute | solution.py:61
  73.2 2.9 collective-permute-done.2
  76.1 3.4 %collective-permute-start.3 = (f32[4,4,2048]{2,1,0:T(4,128)S(1)}, f32[4,4,2048]{2,1,0:T(4,128)S(1)}, u32[]{:S(2)}, u32[]{:S(2)}) collective-permute-start(f32[4,4,2048]{2,1,0:T(4,128)S(1)} %collective-permute-done.2), channel_id=1, source_target_pairs={{0,4},{4,8},{8,12},{12,16},{16,20},{20,24},{24,28},{28,0},{1,5},{5... | collective-permute-start | bytes 393224 | tf_op jit(solution)/shard_map/ppermute | solution.py:61
  79.5 2.5 collective-permute-done.3
  82.0 3.4 %collective-permute-start.4 = (f32[4,4,2048]{2,1,0:T(4,128)S(1)}, f32[4,4,2048]{2,1,0:T(4,128)S(1)}, u32[]{:S(2)}, u32[]{:S(2)}) collective-permute-start(f32[4,4,2048]{2,1,0:T(4,128)S(1)} %collective-permute-done.3), channel_id=1, source_target_pairs={{0,4},{4,8},{8,12},{12,16},{16,20},{20,24},{24,28},{28,0},{1,5},{5... | collective-permute-start | bytes 393224 | tf_op jit(solution)/shard_map/ppermute | solution.py:61
  85.4 2.5 collective-permute-done.4
  87.9 3.3 %collective-permute-start.5 = (f32[4,4,2048]{2,1,0:T(4,128)S(1)}, f32[4,4,2048]{2,1,0:T(4,128)S(1)}, u32[]{:S(2)}, u32[]{:S(2)}) collective-permute-start(f32[4,4,2048]{2,1,0:T(4,128)S(1)} %collective-permute-done.4), channel_id=1, source_target_pairs={{0,4},{4,8},{8,12},{12,16},{16,20},{20,24},{24,28},{28,0},{1,5},{5... | collective-permute-start | bytes 393224 | tf_op jit(solution)/shard_map/ppermute | solution.py:61
  91.2 3.1 collective-permute-done.5
  94.3 3.5 %collective-permute-start.6 = (f32[4,4,2048]{2,1,0:T(4,128)S(1)}, f32[4,4,2048]{2,1,0:T(4,128)S(1)}, u32[]{:S(2)}, u32[]{:S(2)}) collective-permute-start(f32[4,4,2048]{2,1,0:T(4,128)S(1)} %collective-permute-done.5), channel_id=1, source_target_pairs={{0,4},{4,8},{8,12},{12,16},{16,20},{20,24},{24,28},{28,0},{1,5},{5... | collective-permute-start | bytes 393224 | tf_op jit(solution)/shard_map/ppermute | solution.py:61
  97.9 4.5 %collective-permute-done.6 = f32[4,4,2048]{2,1,0:T(4,128)S(1)} collective-permute-done((f32[4,4,2048]{2,1,0:T(4,128)S(1)}, f32[4,4,2048]{2,1,0:T(4,128)S(1)}, u32[]{:S(2)}, u32[]{:S(2)}) %collective-permute-start.6) | collective-permute-done | bytes 131104 | tf_op jit(solution)/shard_map/ppermute | solution.py:61
  102.4 1.2 gather_fusion
  104.0 36.6 %all_gather.6 = bf16[4,4,16384]{2,1,0:T(4,128)(2,1)S(1)} all-gather(bf16[4,4,2048]{2,1,0:T(4,128)(2,1)S(1)} %subtract_convert_fusion.1), channel_id=1, replica_groups=mesh['scan'=8,'bin'=4] {'scan'}, dimensions={2}, use_global_device_ids=true | all-gather | bytes 589824 | tf_op jit(solution)/shard_map/all_gather | solution.py:81
  140.6 36.0 %while.41 = (s32[]{:T(128)}, f32[4,4,512]{2,1,0:T(4,128)S(1)}, s32[]{:T(128)}, s32[8]{0:T(128)S(1)}, s32[8]{0:T(128)S(1)}, /*index=5*/bf16[4,4,16384]{2,1,0:T(4,...) while((s32[]{:T(128)}, f32[4,4,512]{2,1,0:T(4,128)S(1)}, ...), condition=%wide.region_4.5_spmd, body=%wide.region_3.4_spmd.sunk | while | flops 2101261 | bytes 565535 | solution.py:40
  142.5 0.6 dynamic_slice.123
  143.8 1.2 fusion.41
  148.2 1.2 fusion.41
  152.6 1.2 fusion.41
  157.0 1.2 fusion.41
  161.5 1.2 fusion.41
  165.9 1.2 fusion.41
  170.3 1.2 fusion.41
  174.7 1.2 fusion.41
  176.7 5.9 %psum.14 = f32[512]{0:T(512)S(1)} all-reduce(f32[512]{0:T(512)S(1)} %get-tuple-element.217), channel_id=1, replica_groups=mesh['scan'=8,'bin'=4] {'bin'}, use_global_device_ids=true, to_apply=%region_6.7 | all-reduce | flops 512 | bytes 4096 | tf_op jit(solution)/shard_map/psum | solution.py:87
  182.7 36.6 %while.42 = (s32[]{:T(128)}, f32[4,4,16384]{2,1,0:T(4,128)S(1)}, s32[]{:T(128)}, s32[8]{0:T(128)S(1)}, s32[8]{0:T(128)S(1)}, /*index=5*/bf16[4,4,512]{2,1,0:T(4,...) while((s32[]{:T(128)}, f32[4,4,16384]{2,1,0:T(4,128)S(1)}, ...), condition=%wide.region_8.9_spmd, body=%wide.region_7.8_spmd.sunk | while | flops 2101261 | bytes 565535 | solution.py:26
  185.9 1.3 fusion.44
  190.4 1.3 fusion.44
  194.9 1.3 fusion.44
  199.4 1.3 fusion.44
  203.9 1.3 fusion.44
  208.4 1.3 fusion.44
  212.9 1.3 fusion.44
  217.4 1.3 fusion.44
  219.3 1.0 copy.18
  220.4 4.8 %all-to-all-start.1 = ((f32[4,4,8,2048]{3,1,0,2:T(4,128)}), f32[4,4,8,2048]{3,1,0,2:T(4,128)S(1)}, u32[]{:S(2)}, u32[]{:S(2)}) async-start(f32[4,4,8,2048]{3,1,0,2:T(4,128)} %bitcast.56), calls=%async_computation.1 | async-start | bytes 2097152 | tf_op jit(solution)/shard_map/all_to_all | solution.py:78
  225.2 23.2 %all-to-all-done.1 = f32[4,4,8,2048]{3,1,0,2:T(4,128)S(1)} async-done(((f32[4,4,8,2048]{3,1,0,2:T(4,128)}), f32[4,4,8,2048]{3,1,0,2:T(4,128)S(1)}, u32[]{:S(2)}, u32[]{:S(2)}) %all-to-all-start.1) | async-done | bytes 1048608 | tf_op jit(solution)/shard_map/all_to_all | solution.py:78
  248.6 30.7 %all_gather.7 = bf16[4,4,16384]{2,1,0:T(4,128)(2,1)S(1)} all-gather(bf16[4,4,2048]{2,1,0:T(4,128)(2,1)S(1)} %subtract_convert_fusion), channel_id=1, replica_groups=mesh['scan'=8,'bin'=4] {'scan'}, dimensions={2}, use_global_device_ids=true | all-gather | bytes 589824 | tf_op jit(solution)/shard_map/all_gather | solution.py:81
  279.3 36.0 %while.43 = (s32[]{:T(128)}, f32[4,4,512]{2,1,0:T(4,128)S(1)}, s32[]{:T(128)}, s32[8]{0:T(128)S(1)}, s32[8]{0:T(128)S(1)}, /*index=5*/bf16[4,4,16384]{2,1,0:T(4,...) while((s32[]{:T(128)}, f32[4,4,512]{2,1,0:T(4,128)S(1)}, ...), condition=%wide.region_11.12_spmd, body=%wide.region_10.11_spmd.sunk | while | flops 2101261 | bytes 565535 | solution.py:40
  282.5 1.2 fusion.47
  286.9 1.2 fusion.47
  291.4 1.2 fusion.47
  295.8 1.2 fusion.47
  300.2 1.2 fusion.47
  304.6 1.2 fusion.47
  309.1 1.2 fusion.47
  313.5 1.2 fusion.47
  315.4 5.8 %psum.15 = f32[512]{0:T(512)S(1)} all-reduce(f32[512]{0:T(512)S(1)} %multiply_reduce_fusion), channel_id=1, replica_groups=mesh['scan'=8,'bin'=4] {'bin'}, use_global_device_ids=true, to_apply=%region_13.14 | all-reduce | flops 512 | bytes 4096 | tf_op jit(solution)/shard_map/psum | solution.py:87
  321.2 0.6 broadcast_multiply_fusion
  (95 shorter events, 39.9 us)
Async XLA Ops:
  0.0 47.5 %collective-permute-start = (f32[4,4,2048]{2,1,0:T(4,128)}, f32[4,4,2048]{2,1,0:T(4,128)S(1)}, u32[]{:S(2)}, u32[]{:S(2)}) collective-permute-start(f32[4,4,2048]{2,1,0:T(4,128)} %param.19), channel_id=1, source_target_pairs={{0,4},{4,8},{8,12},{12,16},{16,20},{20,24},{24,28},{28,0},{1,5},{5... | collective-permute-start | bytes 393224 | tf_op jit(solution)/shard_map/ppermute | solution.py:61
  3.6 43.1 %copy-start.1 = (f32[4,4,2048]{2,1,0:T(4,128)S(1)}, f32[4,4,2048]{2,1,0:T(4,128)}, u32[]{:S(2)}) copy-start(f32[4,4,2048]{2,1,0:T(4,128)} %param.19) | copy-start | bytes 393220
  41.4 62.3 %all-to-all-start = ((f32[4,4,8,2048]{3,1,0,2:T(4,128)}), f32[4,4,8,2048]{3,1,0,2:T(4,128)S(1)}, u32[]{:S(2)}, u32[]{:S(2)}) async-start(f32[4,4,8,2048]{3,1,0,2:T(4,128)} %bitcast.57), calls=%async_computation | async-start | bytes 2097152 | tf_op jit(solution)/shard_map/all_to_all | solution.py:78
  47.5 20.5 %collective-permute-start.1 = (f32[4,4,2048]{2,1,0:T(4,128)S(1)}, f32[4,4,2048]{2,1,0:T(4,128)S(1)}, u32[]{:S(2)}, u32[]{:S(2)}) collective-permute-start(f32[4,4,2048]{2,1,0:T(4,128)S(1)} %collective-permute-done), channel_id=1, source_target_pairs={{0,4},{4,8},{8,12},{12,16},{16,20},{20,24},{24,28},{28,0},{1,5},{5... | collective-permute-start | bytes 393224 | tf_op jit(solution)/shard_map/ppermute | solution.py:61
  68.0 8.1 %collective-permute-start.2 = (f32[4,4,2048]{2,1,0:T(4,128)S(1)}, f32[4,4,2048]{2,1,0:T(4,128)S(1)}, u32[]{:S(2)}, u32[]{:S(2)}) collective-permute-start(f32[4,4,2048]{2,1,0:T(4,128)S(1)} %collective-permute-done.1), channel_id=1, source_target_pairs={{0,4},{4,8},{8,12},{12,16},{16,20},{20,24},{24,28},{28,0},{1,5},{5... | collective-permute-start | bytes 393224 | tf_op jit(solution)/shard_map/ppermute | solution.py:61
  76.1 5.9 %collective-permute-start.3 = (f32[4,4,2048]{2,1,0:T(4,128)S(1)}, f32[4,4,2048]{2,1,0:T(4,128)S(1)}, u32[]{:S(2)}, u32[]{:S(2)}) collective-permute-start(f32[4,4,2048]{2,1,0:T(4,128)S(1)} %collective-permute-done.2), channel_id=1, source_target_pairs={{0,4},{4,8},{8,12},{12,16},{16,20},{20,24},{24,28},{28,0},{1,5},{5... | collective-permute-start | bytes 393224 | tf_op jit(solution)/shard_map/ppermute | solution.py:61
  82.0 5.9 %collective-permute-start.4 = (f32[4,4,2048]{2,1,0:T(4,128)S(1)}, f32[4,4,2048]{2,1,0:T(4,128)S(1)}, u32[]{:S(2)}, u32[]{:S(2)}) collective-permute-start(f32[4,4,2048]{2,1,0:T(4,128)S(1)} %collective-permute-done.3), channel_id=1, source_target_pairs={{0,4},{4,8},{8,12},{12,16},{16,20},{20,24},{24,28},{28,0},{1,5},{5... | collective-permute-start | bytes 393224 | tf_op jit(solution)/shard_map/ppermute | solution.py:61
  87.9 6.4 %collective-permute-start.5 = (f32[4,4,2048]{2,1,0:T(4,128)S(1)}, f32[4,4,2048]{2,1,0:T(4,128)S(1)}, u32[]{:S(2)}, u32[]{:S(2)}) collective-permute-start(f32[4,4,2048]{2,1,0:T(4,128)S(1)} %collective-permute-done.4), channel_id=1, source_target_pairs={{0,4},{4,8},{8,12},{12,16},{16,20},{20,24},{24,28},{28,0},{1,5},{5... | collective-permute-start | bytes 393224 | tf_op jit(solution)/shard_map/ppermute | solution.py:61
  94.3 8.0 %collective-permute-start.6 = (f32[4,4,2048]{2,1,0:T(4,128)S(1)}, f32[4,4,2048]{2,1,0:T(4,128)S(1)}, u32[]{:S(2)}, u32[]{:S(2)}) collective-permute-start(f32[4,4,2048]{2,1,0:T(4,128)S(1)} %collective-permute-done.5), channel_id=1, source_target_pairs={{0,4},{4,8},{8,12},{12,16},{16,20},{20,24},{24,28},{28,0},{1,5},{5... | collective-permute-start | bytes 393224 | tf_op jit(solution)/shard_map/ppermute | solution.py:61
  103.5 73.1 %copy-start = (f32[4,4,512]{2,1,0:T(4,128)S(1)}, f32[4,4,512]{2,1,0:T(4,128)}, u32[]{:S(2)}) copy-start(f32[4,4,512]{2,1,0:T(4,128)} %param.18) | copy-start | bytes 98308
  103.6 79.0 %copy-start.2 = (f32[512]{0:T(512)S(1)}, f32[512]{0:T(512)}, u32[]{:S(2)}) copy-start(f32[512]{0:T(512)} %param.21) | copy-start | bytes 6148
  220.4 28.0 %all-to-all-start.1 = ((f32[4,4,8,2048]{3,1,0,2:T(4,128)}), f32[4,4,8,2048]{3,1,0,2:T(4,128)S(1)}, u32[]{:S(2)}, u32[]{:S(2)}) async-start(f32[4,4,8,2048]{3,1,0,2:T(4,128)} %bitcast.56), calls=%async_computation.1 | async-start | bytes 2097152 | tf_op jit(solution)/shard_map/all_to_all | solution.py:78
